TPU v7x, 32 devices: a whole 2x2x4 slice. The times are simulated.
32 devices in a mesh: dp: 8 (over y, x, core), mp: 4 (over z).
Axes of the slice: x: 2, y: 2, z: 4, core: 2. Of those that a mesh axis runs over, the one named last changes fastest.
Arguments:
- frames: bfloat16 [16384, 640], P('dp'), may hold values from -6 to 6
- seg_ids: int32 [16384], P('dp'), may hold values from 0 to 15, as said below
- qkv_weight: bfloat16 [3, 640, 768], P(None, 'dp', 'mp'), may hold values from -0.25 to 0.25
- qkv_bias: float32 [2, 768], P(None, 'mp'), may hold values from -3 to 3
- out_weight: bfloat16 [768, 640], P('mp', 'dp'), may hold values from -1.5 to 1.5
- out_bias: float32 [640], replicated, may hold values from -3 to 3
- gain_one: float32 [640], replicated, may hold values from 0.1 to 1.9
- shift_one: float32 [640], replicated, may hold values from -3 to 3
- up_weight: bfloat16 [640, 2240], P('dp', 'mp'), may hold values from -0.25 to 0.25
- up_bias: float32 [2240], P('mp'), may hold values from -3 to 3
- down_weight: bfloat16 [2240, 640], P('mp', 'dp'), may hold values from -0.125 to 0.125
- down_bias: float32 [640], replicated, may hold values from -3 to 3
- gain_two: float32 [640], replicated, may hold values from 0.1 to 1.9
- shift_two: float32 [640], replicated, may hold values from -3 to 3
- cotangent: bfloat16 [16384, 640], P('dp'), may hold values from -6 to 6
Outputs:
- output_frames: bfloat16 [16384, 640], P(('dp', 'mp'))
- frames_grad: bfloat16 [16384, 640], P(('dp', 'mp'))
- qkv_grad: float32 [3, 640, 768], P(None, 'dp', 'mp')
- qkv_bias_grad: float32 [2, 768], P(None, 'mp')
- out_grad: float32 [768, 640], P('mp', 'dp')
- out_bias_grad: float32 [640], replicated
- gain_one_grad: float32 [640], replicated
- shift_one_grad: float32 [640], replicated
- up_grad: float32 [640, 2240], P('dp', 'mp')
- up_bias_grad: float32 [2240], P('mp')
- down_grad: float32 [2240, 640], P('mp', 'dp')
- down_bias_grad: float32 [640], replicated
- gain_two_grad: float32 [640], replicated
- shift_two_grad: float32 [640], replicated
Inputs may be any that keep to these rules, and one draw needn't show every extreme that they name: `seg_ids`: each block of 2048 frames that one index of dp holds contains 1 to 16 whole utterances laid end to end; within the block the number starts at 0 and rises by one at each new utterance. In every draw some block holds a single utterance of 2048 frames and some block holds 16 utterances.
All inputs are finite; a program needn't handle non-finite values.
Results may differ from a plain program's by a relative error of at most 0.019.
Values may be sent and summed in bfloat16 or wider, within the bound.
A program may use at most 192 MiB of HBM per device.

v0:
```python
import jax
import jax.numpy as jnp
from jax import lax
from jax.sharding import PartitionSpec as P

HEADS = 10
HD = 64
EPS = 1e-05
SCALE = 0.125


def cut_along(array, dim, length):
    before, after = (array.shape[:dim], array.shape[dim + 1 :])
    return jnp.moveaxis(array.reshape(*before, length, -1, *after), dim, 0)


def sum_at_owner(array, axis, dim):
    parts = cut_along(array, dim, lax.axis_size(axis))
    arrived = lax.all_to_all(parts, axis, split_axis=0, concat_axis=0, tiled=True)
    return arrived.astype(jnp.float32).sum(axis=0)


def norm_forward(summed):
    centre = summed - jnp.mean(summed, -1, keepdims=True)
    spread = jnp.mean(centre * centre, -1, keepdims=True)
    factor = lax.rsqrt(spread + EPS)
    return (centre * factor, factor)


def norm_backward(upper, normed, factor, gain):
    scaled = upper * gain
    return factor * (
        scaled
        - jnp.mean(scaled, -1, keepdims=True)
        - normed * jnp.mean(scaled * normed, -1, keepdims=True)
    )


def gelu_exact(values):
    return jax.nn.gelu(values, approximate=False)


def body(
    frames,
    seg_ids,
    qkv_weight,
    qkv_bias,
    out_weight,
    out_bias,
    gain_one,
    shift_one,
    up_weight,
    up_bias,
    down_weight,
    down_bias,
    gain_two,
    shift_two,
    cotangent,
):
    qkv_full, out_full, up_full, down_full = (
        lax.all_gather(qkv_weight, "dp", axis=1, tiled=True),
        lax.all_gather(out_weight, "dp", axis=1, tiled=True),
        lax.all_gather(up_weight, "dp", axis=0, tiled=True),
        lax.all_gather(down_weight, "dp", axis=1, tiled=True),
    )
    total_rows = frames.shape[0]
    mp_size = lax.axis_size("mp")
    mp_index = lax.axis_index("mp")
    share_rows = total_rows // mp_size
    share_start = mp_index * share_rows
    slot_count = qkv_weight.shape[2] // HD
    hidden_cols = up_weight.shape[1]
    live_count = HEADS // mp_size + (mp_index < HEADS % mp_size).astype(jnp.int32)
    live_mask = (jnp.arange(slot_count) < live_count).astype(jnp.float32)
    live_low = live_mask.astype(jnp.bfloat16)
    projected = jnp.einsum("rd,ids->irs", frames, qkv_full, preferred_element_type=jnp.float32)
    offsets = jnp.stack([qkv_bias[0], jnp.zeros_like(qkv_bias[0]), qkv_bias[1]])
    head_values = (
        (projected + offsets[:, None, :])
        .astype(jnp.bfloat16)
        .reshape(3, total_rows, slot_count, HD)
    )
    queries = head_values[0]
    keys_all = head_values[1]
    values = head_values[2]
    block_rows = min(512, total_rows)
    block_count = total_rows // block_rows

    def scores_at(anchor):
        query_block = lax.dynamic_slice_in_dim(queries, anchor, block_rows, 0)
        seg_block = lax.dynamic_slice_in_dim(seg_ids, anchor, block_rows, 0)
        raw_scores = (
            jnp.einsum("qhd,khd->hqk", query_block, keys_all, preferred_element_type=jnp.float32)
            * SCALE
        )
        same_utter = seg_block[:, None] == seg_ids[None, :]
        return (query_block, jnp.where(same_utter[None], raw_scores, -1e30))

    def attend(position):
        unused, scores = scores_at(position * block_rows)
        maxima = jnp.max(scores, -1, keepdims=True)
        raised = jnp.exp(scores - maxima)
        totals = jnp.sum(raised, -1, keepdims=True)
        prob_low = (raised / totals).astype(jnp.bfloat16)
        mixed = jnp.einsum("hqk,khd->qhd", prob_low, values, preferred_element_type=jnp.float32)
        return (mixed, maxima, totals)

    attended, all_maxima, all_totals = lax.map(attend, jnp.arange(block_count))
    attended = attended.reshape(total_rows, slot_count, HD) * live_mask[None, :, None]
    mixed_low = attended.reshape(total_rows, slot_count * HD).astype(jnp.bfloat16)
    frames_wide = frames.astype(jnp.float32)

    def share_of(array):
        return lax.dynamic_slice_in_dim(array, share_start, share_rows, 0)

    attention = lax.psum(
        jnp.dot(mixed_low, out_full, preferred_element_type=jnp.float32).astype(jnp.bfloat16), "mp"
    ).astype(jnp.float32)
    normed_one, factor_one = norm_forward(frames_wide + attention + out_bias)
    hidden = normed_one * gain_one + shift_one
    hidden_low = hidden.astype(jnp.bfloat16)
    act_low = gelu_exact(
        jnp.dot(hidden_low, up_full, preferred_element_type=jnp.float32) + up_bias
    ).astype(jnp.bfloat16)
    feed = lax.psum(
        jnp.dot(act_low, down_full, preferred_element_type=jnp.float32).astype(jnp.bfloat16), "mp"
    ).astype(jnp.float32)
    normed_two, factor_two = norm_forward(hidden + feed + down_bias)
    output_frames = share_of(normed_two * gain_two + shift_two).astype(jnp.bfloat16)
    upstream = cotangent.astype(jnp.float32)
    sum_two_grad = norm_backward(upstream, normed_two, factor_two, gain_two)
    sum_two_low = sum_two_grad.astype(jnp.bfloat16)
    pre_act = jnp.dot(hidden_low, up_full, preferred_element_type=jnp.float32) + up_bias
    activation, pullback = jax.vjp(gelu_exact, pre_act)
    act_low = activation.astype(jnp.bfloat16)
    grad_down = jnp.einsum("rf,rd->fd", act_low, sum_two_low, preferred_element_type=jnp.float32)
    act_grad = jnp.einsum("rd,fd->rf", sum_two_low, down_full, preferred_element_type=jnp.float32)
    pre_low = pullback(act_grad)[0].astype(jnp.bfloat16)
    grad_up = jnp.einsum("rd,rf->df", hidden_low, pre_low, preferred_element_type=jnp.float32)
    bias_up = jnp.sum(pre_low.astype(jnp.float32), 0)
    grad_up, bias_up, grad_down, pre_low = (grad_up, bias_up, grad_down, pre_low)
    hidden_part = jnp.einsum("rf,df->rd", pre_low, up_full, preferred_element_type=jnp.float32)
    hidden_grad = (
        lax.psum(hidden_part.astype(jnp.bfloat16), "mp").astype(jnp.float32) + sum_two_grad
    )
    sum_one_grad = norm_backward(hidden_grad, normed_one, factor_one, gain_one)
    sum_one_low = sum_one_grad.astype(jnp.bfloat16)
    grad_proj = jnp.einsum("rs,rd->sd", mixed_low, sum_one_low, preferred_element_type=jnp.float32)
    back_mixed = jnp.einsum("rd,sd->rs", sum_one_low, out_full, preferred_element_type=jnp.float32)
    back_mixed = (
        back_mixed.astype(jnp.bfloat16).reshape(total_rows, slot_count, HD)
        * live_low[None, :, None]
    )

    def step(running, record):
        key_grad, value_grad = running
        position, maxima, totals = record
        anchor = position * block_rows
        query_block, scores = scores_at(anchor)
        probs = jnp.exp(scores - maxima) / totals
        prob_low = probs.astype(jnp.bfloat16)
        back_block = lax.dynamic_slice_in_dim(back_mixed, anchor, block_rows, 0)
        value_grad = value_grad + jnp.einsum(
            "hqk,qhd->khd", prob_low, back_block, preferred_element_type=jnp.float32
        )
        prob_grad = jnp.einsum(
            "qhd,khd->hqk", back_block, values, preferred_element_type=jnp.float32
        )
        score_low = (probs * (prob_grad - jnp.sum(probs * prob_grad, -1, keepdims=True))).astype(
            jnp.bfloat16
        )
        query_grad = (
            jnp.einsum("hqk,khd->qhd", score_low, keys_all, preferred_element_type=jnp.float32)
            * SCALE
        )
        key_grad = (
            key_grad
            + jnp.einsum("hqk,qhd->khd", score_low, query_block, preferred_element_type=jnp.float32)
            * SCALE
        )
        return ((key_grad, value_grad), query_grad)

    zeros = jnp.zeros((total_rows, slot_count, HD), jnp.float32)
    (key_grad, value_grad), query_grad = lax.scan(
        step, (zeros, zeros), (jnp.arange(block_count), all_maxima, all_totals)
    )
    query_grad = query_grad.reshape(total_rows, slot_count, HD)
    grads_low = (
        jnp.stack([query_grad, key_grad, value_grad])
        .reshape(3, total_rows, slot_count * HD)
        .astype(jnp.bfloat16)
    )
    grad_qkv = jnp.einsum("rd,irs->ids", frames, grads_low, preferred_element_type=jnp.float32)
    bias_qkv = jnp.stack(
        [jnp.sum(grads_low[0].astype(jnp.float32), 0), jnp.sum(grads_low[2].astype(jnp.float32), 0)]
    )
    grad_qkv, bias_qkv, grad_proj, grads_low = (grad_qkv, bias_qkv, grad_proj, grads_low)
    input_part = jnp.einsum("irs,ids->rd", grads_low, qkv_full, preferred_element_type=jnp.float32)
    input_grad = lax.psum(input_part.astype(jnp.bfloat16), "mp").astype(jnp.float32) + sum_one_grad
    frames_grad = share_of(input_grad).astype(jnp.bfloat16)
    upstream_share = share_of(upstream)
    hidden_share = share_of(hidden_grad)
    out_bias_term = jnp.sum(share_of(sum_one_low).astype(jnp.float32), 0)
    gain_one_term = jnp.sum(hidden_share * share_of(normed_one), 0)
    shift_one_term = jnp.sum(hidden_share, 0)
    down_bias_term = jnp.sum(share_of(sum_two_low).astype(jnp.float32), 0)
    gain_two_term = jnp.sum(upstream_share * share_of(normed_two), 0)
    shift_two_term = jnp.sum(upstream_share, 0)
    matrix_grads = (
        sum_at_owner(grad_qkv.astype(jnp.bfloat16), "dp", 1),
        sum_at_owner(grad_proj.astype(jnp.bfloat16), "dp", 1),
        sum_at_owner(grad_up.astype(jnp.bfloat16), "dp", 0),
        sum_at_owner(grad_down.astype(jnp.bfloat16), "dp", 1),
    )
    slot_width = slot_count * HD
    padded_qkv = lax.dynamic_update_slice(
        jnp.zeros((2, mp_size * slot_width), jnp.float32), bias_qkv, (0, mp_index * slot_width)
    )
    padded_up = lax.dynamic_update_slice(
        jnp.zeros((mp_size * hidden_cols,), jnp.float32), bias_up, (mp_index * hidden_cols,)
    )
    summed = lax.psum(
        (
            padded_qkv,
            padded_up,
            out_bias_term,
            gain_one_term,
            shift_one_term,
            down_bias_term,
            gain_two_term,
            shift_two_term,
        ),
        ("dp", "mp"),
    )
    qkv_bias_grad = lax.dynamic_slice_in_dim(summed[0], mp_index * slot_width, slot_width, 1)
    up_bias_grad = lax.dynamic_slice_in_dim(summed[1], mp_index * hidden_cols, hidden_cols, 0)
    return (
        output_frames,
        frames_grad,
        matrix_grads[0],
        qkv_bias_grad,
        matrix_grads[1],
        summed[2],
        summed[3],
        summed[4],
        matrix_grads[2],
        up_bias_grad,
        matrix_grads[3],
        summed[5],
        summed[6],
        summed[7],
    )


def solution(mesh):
    in_specs = (
        P("dp", None),
        P("dp"),
        P(None, "dp", "mp"),
        P(None, "mp"),
        P("mp", "dp"),
        P(),
        P(),
        P(),
        P("dp", "mp"),
        P("mp"),
        P("mp", "dp"),
        P(),
        P(),
        P(),
        P("dp", None),
    )
    out_specs = (
        P(("dp", "mp"), None),
        P(("dp", "mp"), None),
        P(None, "dp", "mp"),
        P(None, "mp"),
        P("mp", "dp"),
        P(),
        P(),
        P(),
        P("dp", "mp"),
        P("mp"),
        P("mp", "dp"),
        P(),
        P(),
        P(),
    )
    return jax.shard_map(body, mesh=mesh, in_specs=in_specs, out_specs=out_specs, check_vma=False)
```

profile of v0, /device:TPU:0, one launch (start us, length us, event | category | flops | bytes accessed | tf_op | source)
XLA Modules:
  0.0 783.6 jit_solution(1316347857595142371)
XLA Ops:
  8.2 11.1 %all_gather.13 = bf16[192,640]{0,1:T(8,128)(2,1)S(1)} all-gather(bf16[192,80]{0,1:T(8,128)(2,1)} %param.23), channel_id=1, replica_groups=mesh['dp'=8,'mp'=4] {'dp'}, dimensions={1}, use_global_device_ids=true | all-gather | bytes 276480 | tf_op jit(solution)/shard_map/all_gather | solution.py:62
  19.3 10.8 %all_gather.12 = bf16[3,640,192]{2,1,0:T(8,128)(2,1)S(1)} all-gather(bf16[3,80,192]{2,1,0:T(8,128)(2,1)} %param.21), channel_id=1, replica_groups=mesh['dp'=8,'mp'=4] {'dp'}, dimensions={1}, use_global_device_ids=true | all-gather | bytes 829440 | tf_op jit(solution)/shard_map/all_gather | solution.py:61
  30.2 4.4 fusion.38
  35.3 124.3 %while.29 = (s32[]{:T(128)}, f32[4,512,3,64]{1,0,3,2:T(4,128)}, f32[4,3,512,1]{2,1,3,0:T(4,128)}, f32[4,3,512,1]{2,1,3,0:T(4,128)S(1)}, s32[4]{0:T(128)S(1)}, /*...) while((s32[]{:T(128)}, f32[4,512,3,64]{1,0,3,2:T(4,128)}, ...), condition=%wide.region_3.4_spmd, body=%wide.region_0.3_spmd.sunk | while | flops 844100608 | bytes 45756624 | solution.py:108
  37.3 6.0 fusion.104
  43.3 6.8 fusion.105
  50.1 6.7 fusion.106
  57.8 8.6 %dynamic_update_slice.30 = f32[4,512,3,64]{1,0,3,2:T(4,128)} dynamic-update-slice(f32[4,512,3,64]{1,0,3,2:T(4,128)} %get-tuple-element.413, f32[1,512,3,64]{1,0,3,2:T(1,128)S(1)} %copy.68, s32[]{:T(128)S(6)} %copy.77, s32[]{:T(128)} %constant.76.clone.1..sunk, s32[]{:T(128)} %constant.76.clone.1..sunk, s32[]{:T(128)} %constant.76.clone.1..sunk) | dynamic-update-slice | bytes 786436 | tf_op jit(solution)/shard_map/while/body/jit(dynamic_update_index_in_dim)/dynamic_update_slice | solution.py:108
  68.4 6.0 fusion.104
  74.4 6.8 fusion.105
  81.2 6.7 fusion.106
  88.9 8.6 %dynamic_update_slice.30 = f32[4,512,3,64]{1,0,3,2:T(4,128)} dynamic-update-slice(f32[4,512,3,64]{1,0,3,2:T(4,128)} %get-tuple-element.413, f32[1,512,3,64]{1,0,3,2:T(1,128)S(1)} %copy.68, s32[]{:T(128)S(6)} %copy.77, s32[]{:T(128)} %constant.76.clone.1..sunk, s32[]{:T(128)} %constant.76.clone.1..sunk, s32[]{:T(128)} %constant.76.clone.1..sunk) | dynamic-update-slice | bytes 786436 | tf_op jit(solution)/shard_map/while/body/jit(dynamic_update_index_in_dim)/dynamic_update_slice | solution.py:108
  99.5 6.0 fusion.104
  105.5 6.8 fusion.105
  112.3 6.7 fusion.106
  119.9 8.6 %dynamic_update_slice.30 = f32[4,512,3,64]{1,0,3,2:T(4,128)} dynamic-update-slice(f32[4,512,3,64]{1,0,3,2:T(4,128)} %get-tuple-element.413, f32[1,512,3,64]{1,0,3,2:T(1,128)S(1)} %copy.68, s32[]{:T(128)S(6)} %copy.77, s32[]{:T(128)} %constant.76.clone.1..sunk, s32[]{:T(128)} %constant.76.clone.1..sunk, s32[]{:T(128)} %constant.76.clone.1..sunk) | dynamic-update-slice | bytes 786436 | tf_op jit(solution)/shard_map/while/body/jit(dynamic_update_index_in_dim)/dynamic_update_slice | solution.py:108
  130.5 6.0 fusion.104
  136.6 6.8 fusion.105
  143.3 6.7 fusion.106
  151.0 8.6 %dynamic_update_slice.30 = f32[4,512,3,64]{1,0,3,2:T(4,128)} dynamic-update-slice(f32[4,512,3,64]{1,0,3,2:T(4,128)} %get-tuple-element.413, f32[1,512,3,64]{1,0,3,2:T(1,128)S(1)} %copy.68, s32[]{:T(128)S(6)} %copy.77, s32[]{:T(128)} %constant.76.clone.1..sunk, s32[]{:T(128)} %constant.76.clone.1..sunk, s32[]{:T(128)} %constant.76.clone.1..sunk) | dynamic-update-slice | bytes 786436 | tf_op jit(solution)/shard_map/while/body/jit(dynamic_update_index_in_dim)/dynamic_update_slice | solution.py:108
  166.6 11.7 %all_gather.14 = bf16[640,560]{1,0:T(8,128)(2,1)} all-gather(bf16[80,560]{1,0:T(8,128)(2,1)S(1)} %copy-done.29), channel_id=1, replica_groups=mesh['dp'=8,'mp'=4] {'dp'}, dimensions={0}, use_global_device_ids=true | all-gather | bytes 806400 | tf_op jit(solution)/shard_map/all_gather | solution.py:63
  178.3 11.1 %all_gather.15 = bf16[560,640]{0,1:T(8,128)(2,1)} all-gather(bf16[560,80]{0,1:T(8,128)(2,1)S(1)} %copy-done.30), channel_id=1, replica_groups=mesh['dp'=8,'mp'=4] {'dp'}, dimensions={1}, use_global_device_ids=true | all-gather | bytes 806400 | tf_op jit(solution)/shard_map/all_gather | solution.py:64
  189.4 81.7 %all-reduce.6.cloned.1.call-done = bf16[2048,640]{1,0:T(8,128)(2,1)} async-done(((bf16[2048,640]{1,0:T(8,128)(2,1)}), bf16[2048,640]{1,0:T(8,128)(2,1)}) %all-reduce.6.cloned.1.call-update) | async-done | bytes 2621456 | tf_op jit(solution)/shard_map/psum | solution.py:116
  271.0 3.6 fusion.37
  277.4 13.3 %multiply_convert_fusion.1 = (bf16[2048,560]{0,1:T(8,128)(2,1)S(1)}, f32[2048,560]{0,1:T(8,128)}, f32[2048,560]{0,1:T(8,128)}) fusion(f32[560]{0:T(1024)S(1)} %copy-done.44, bf16[640,560]{1,0:T(8,128)(2,1)S(1)} %copy-done.23, f32[2048,640]{1,0:T(8,128)S(1)} %subtract_multiply_fusion.3, f32[640]{0:T(1024)S(1)} %copy-done.36, f32[640]{0:T(1024)S(1)} %copy-done.31), kind=kOutput, calls=%fused_computation.61 | convolution fusion | flops 1547632640 | bytes 17435840 | tf_op jit(solution)/shard_map/dot_general | solution.py:123
  292.1 3.9 convolution_convert_fusion.1
  296.3 103.0 %all-reduce.8.cloned.1.call-done = bf16[2048,640]{1,0:T(8,128)(2,1)} async-done(((bf16[2048,640]{1,0:T(8,128)(2,1)}), bf16[2048,640]{1,0:T(8,128)(2,1)}) %all-reduce.8.cloned.1.call-update) | async-done | bytes 2621456 | tf_op jit(solution)/shard_map/psum | solution.py:125
  399.3 4.5 fusion.52
  403.9 3.5 multiply_reduce_fusion.3
  413.3 4.5 convert_reduce_fusion
  419.2 4.0 convolution_convert_fusion
  423.7 5.2 convolution_convert_fusion.5
  431.2 4.2 all-to-all-start.3
  435.9 90.5 %all-reduce.10.cloned.1.call-done = bf16[2048,640]{1,0:T(8,128)(2,1)} async-done(((bf16[2048,640]{1,0:T(8,128)(2,1)}), bf16[2048,640]{1,0:T(8,128)(2,1)}) %all-reduce.10.cloned.1.call-update) | async-done | bytes 2621456 | tf_op jit(solution)/shard_map/psum | solution.py:144
  526.4 7.0 multiply_reduce_fusion.5
  533.5 6.6 fusion.57
  543.7 114.9 %while.30 = (s32[]{:T(128)}, f32[2048,3,64]{0,2,1:T(8,128)S(1)}, f32[2048,3,64]{0,2,1:T(8,128)S(1)}, bf16[4,512,3,64]{1,3,2,0:T(8,128)(2,1)}, s32[4]{0:T(128)S(1...) while((s32[]{:T(128)}, f32[2048,3,64]{0,2,1:T(8,128)S(1)}, ...), condition=%wide.region_17.18_spmd.clone, body=%wide.region_15.17_spmd.clone.sunk | while | flops 2047834624 | bytes 118950256 | solution.py:184
  546.4 3.2 fusion.116
  549.6 7.7 multiply_reduce_fusion.10
  557.3 5.5 multiply_convert_fusion.6
  562.8 6.2 fusion.118
  575.1 3.2 fusion.116
  578.3 7.7 multiply_reduce_fusion.10
  586.0 5.5 multiply_convert_fusion.6
  591.5 6.2 fusion.118
  603.9 3.2 fusion.116
  607.1 7.7 multiply_reduce_fusion.10
  614.8 5.5 multiply_convert_fusion.6
  620.2 6.2 fusion.118
  632.6 3.2 fusion.116
  635.8 7.7 multiply_reduce_fusion.10
  643.5 5.5 multiply_convert_fusion.6
  649.0 6.2 fusion.118
  666.2 4.0 bitcast_convert_fusion
  670.3 4.5 convolution_convert_fusion.4
  676.0 3.8 all-to-all-start.2
  682.8 3.0 dynamic-slice_reduce_fusion
  687.8 5.0 all-to-all-done.2
  693.6 3.0 convolution_convert_fusion.6
  698.5 4.1 all-to-all-start.1
  702.6 5.1 fusion.46
  712.2 4.2 all-to-all-start
  721.3 44.5 %all-reduce = (f32[2,768]{1,0:T(2,128)S(1)}, f32[640]{0:T(1024)}, f32[640]{0:T(1024)}, f32[640]{0:T(1024)}, f32[2240]{0:T(1024)S(1)}, /*index=5*/f32[640]{0:T(1024)}, f32[640]{0:T(1024)}, f32[640]{0:T(1024)}) all-reduce(f32[2,768]{1,0:T(2,128)S(1)} %dynamic_update_slice.20, ...), channel_id=1, replica_groups=mesh['dp'=8,'mp'=4] {'dp','mp'}, use_global_device_ids=true, to_apply=%region_22.23 | all-reduce | flops 7616 | bytes 60928 | tf_op jit(solution)/shard_map/psum | solution.py:222
  770.9 3.6 all-reduce.12.cloned.1.call-done
  (248 shorter events, 91.4 us)
Async XLA Ops:
  7.2 263.9 %all-reduce.6.cloned.1.call-start = ((), (), s32[]{:S(2)}) async-start(), calls=%async_computation.4 | async-start | bytes 5242880 | tf_op jit(solution)/shard_map/psum | solution.py:116
  7.4 155.2 %copy-start.39 = (f32[192]{0:T(256)}, f32[192]{0:T(256)S(1)}, u32[]{:S(2)}) copy-start(f32[192]{0:T(256)S(1)} %mul.192) | copy-start | bytes 2308
  30.1 4.6 copy-start.21
  159.6 6.8 copy-start.2
  159.6 6.8 copy-start.5
  159.6 6.8 copy-start.15
  159.6 6.9 copy-start.29
  162.6 15.7 %copy-start.30 = (bf16[560,80]{0,1:T(8,128)(2,1)S(1)}, bf16[560,80]{0,1:T(8,128)(2,1)}, u32[]{:S(2)}) copy-start(bf16[560,80]{0,1:T(8,128)(2,1)} %param.29) | copy-start | bytes 268804
  162.6 108.5 %copy-start.38 = (f32[640]{0:T(1024)S(1)}, f32[640]{0:T(1024)}, u32[]{:S(2)}) copy-start(f32[640]{0:T(1024)} %param.24) | copy-start | bytes 7684
  166.5 232.8 %all-reduce.8.cloned.1.call-start = ((), (), s32[]{:S(2)}) async-start(), calls=%async_computation.5 | async-start | bytes 5242880 | tf_op jit(solution)/shard_map/psum | solution.py:125
  166.5 108.1 %copy-start.11 = (bf16[2048,640]{1,0:T(8,128)(2,1)S(1)}, bf16[2048,640]{1,0:T(8,128)(2,1)}, u32[]{:S(2)}) copy-start(bf16[2048,640]{1,0:T(8,128)(2,1)} %param.19) | copy-start | bytes 7864324
  271.0 3.6 copy-start.12
  277.3 13.3 %copy-start = (f32[2048,640]{1,0:T(8,128)}, f32[2048,640]{1,0:T(8,128)S(1)}, u32[]{:S(2)}) copy-start(f32[2048,640]{1,0:T(8,128)S(1)} %subtract_multiply_fusion.3) | copy-start | bytes 15728644
  277.3 14.8 %copy-start.25 = (bf16[560,640]{0,1:T(8,128)(2,1)S(1)}, bf16[560,640]{0,1:T(8,128)(2,1)}, u32[]{:S(2)}) copy-start(bf16[560,640]{0,1:T(8,128)(2,1)} %all_gather.15) | copy-start | bytes 2150404
  290.7 1.4 copy-start.45
  292.1 107.2 %copy-start.35 = (f32[640]{0:T(1024)S(1)}, f32[640]{0:T(1024)}, u32[]{:S(2)}) copy-start(f32[640]{0:T(1024)} %param.30) | copy-start | bytes 7684
  296.0 230.4 %all-reduce.10.cloned.1.call-start = ((), (), s32[]{:S(2)}) async-start(), calls=%async_computation.6 | async-start | bytes 5242880 | tf_op jit(solution)/shard_map/psum | solution.py:144
  399.3 4.6 copy-start.10
  399.3 8.1 %slice-start = ((s8[5242880]{0:T(1024)(128)(4,1)}), s8[1048576]{0:T(1024)(128)(4,1)S(1)}, s32[]{:S(2)}) async-start(s8[5242880]{0:T(1024)(128)(4,1)} %bitcast.122), calls=%async_computation.8 | async-start | bytes 2097152
  403.9 3.6 copy-start.3
  403.9 3.6 copy-start.33
  403.9 4.5 slice-start.1
  403.9 9.3 %slice-start.2 = ((s8[4587520]{0:T(1024)(128)(4,1)}), s8[4194304]{0:T(1024)(128)(4,1)S(1)}, s32[]{:S(2)}) async-start(s8[4587520]{0:T(1024)(128)(4,1)} %bitcast.141), calls=%async_computation.10 | async-start | bytes 8388608
  403.9 9.3 %slice-start.4 = ((s8[4587520]{0:T(1024)(128)(4,1)}), s8[4194304]{0:T(1024)(128)(4,1)S(1)}, s32[]{:S(2)}) async-start(s8[4587520]{0:T(1024)(128)(4,1)} %bitcast.143), calls=%async_computation.12 | async-start | bytes 8388608
  408.4 4.8 slice-start.3
  408.4 4.8 slice-start.5
  410.9 2.3 copy-start.1
  413.2 4.6 copy-start.14
  413.2 5.9 copy-start.24
  431.2 244.8 %all-to-all-start.3 = ((bf16[8,560,80]{1,2,0:T(8,128)(2,1)}), bf16[8,560,80]{1,2,0:T(8,128)(2,1)}, u32[]{:S(2)}, u32[]{:S(2)}) async-start(bf16[8,560,80]{1,2,0:T(8,128)(2,1)} %bitcast.130), calls=%async_computation.3 | async-start | bytes 1638400 | tf_op jit(solution)/shard_map/all_to_all | solution.py:19
  435.4 339.0 %all-reduce.12.cloned.1.call-start = ((), (), s32[]{:S(2)}) async-start(), calls=%async_computation.7 | async-start | bytes 5242880 | tf_op jit(solution)/shard_map/psum | solution.py:199
  533.4 6.6 copy-start.9
  533.4 9.2 %copy-start.43 = (bf16[3]{0:T(256)(128)(2,1)S(1)}, bf16[3]{0:T(256)(128)(2,1)}, u32[]{:S(2)}) copy-start(bf16[3]{0:T(256)(128)(2,1)} %fusion.55) | copy-start | bytes 22
  540.0 1.5 copy-start.7
  546.4 3.2 copy-start.6
  546.4 3.2 copy-start.16
  562.8 6.2 copy-start.26
  571.0 1.4 copy-start.27
  575.1 3.2 copy-start.6
  575.1 3.2 copy-start.16
  591.5 6.2 copy-start.26
  599.7 1.4 copy-start.27
  603.8 3.2 copy-start.6
  603.9 3.2 copy-start.16
  620.2 6.2 copy-start.26
  628.5 1.4 copy-start.27
  632.6 3.2 copy-start.6
  632.6 3.2 copy-start.16
  649.0 6.2 copy-start.26
  657.2 1.4 copy-start.27
  664.2 2.0 copy-start.22
  666.2 4.0 copy-start.32
  666.2 4.0 copy-start.37
  666.2 4.1 copy-start.47
  674.8 5.1 copy-start.4
  676.0 6.5 copy-start.42
  676.0 6.8 copy-start.34
  676.0 6.8 copy-start.41
  676.0 16.8 %all-to-all-start.2 = ((bf16[8,80,560]{2,1,0:T(8,128)(2,1)}), bf16[8,80,560]{2,1,0:T(8,128)(2,1)S(1)}, u32[]{:S(2)}, u32[]{:S(2)}) async-start(bf16[8,80,560]{2,1,0:T(8,128)(2,1)} %bitcast.21), calls=%async_computation.2 | async-start | bytes 1638400 | tf_op jit(solution)/shard_map/all_to_all | solution.py:19
  682.5 11.1 %copy-start.8 = (bf16[2048,640]{1,0:T(8,128)(2,1)S(1)}, bf16[2048,640]{1,0:T(8,128)(2,1)}, u32[]{:S(2)}) copy-start(bf16[2048,640]{1,0:T(8,128)(2,1)} %copy-done.7) | copy-start | bytes 7864324
  682.5 11.1 %copy-start.40 = (f32[192]{0:T(256)S(1)}, f32[192]{0:T(256)}, u32[]{:S(2)}) copy-start(f32[192]{0:T(256)} %copy-done.39) | copy-start | bytes 2308
  693.6 8.9 %copy-start.18 = (bf16[1,2048,192]{1,2,0:T(8,128)(2,1)S(1)}, bf16[1,2048,192]{1,2,0:T(8,128)(2,1)}, u32[]{:S(2)}) copy-start(bf16[1,2048,192]{1,2,0:T(8,128)(2,1)} %stack.24) | copy-start | bytes 2359300
  698.5 13.7 %all-to-all-start.1 = ((bf16[8,192,80]{1,2,0:T(8,128)(2,1)}), bf16[8,192,80]{1,2,0:T(8,128)(2,1)}, u32[]{:S(2)}, u32[]{:S(2)}) async-start(bf16[8,192,80]{1,2,0:T(8,128)(2,1)} %bitcast.136), calls=%async_computation.1 | async-start | bytes 655360 | tf_op jit(solution)/shard_map/all_to_all | solution.py:19
  712.2 56.7 %all-to-all-start = ((bf16[8,3,80,192]{3,2,1,0:T(8,128)(2,1)}), bf16[8,3,80,192]{3,2,1,0:T(8,128)(2,1)}, u32[]{:S(2)}, u32[]{:S(2)}) async-start(bf16[8,3,80,192]{3,2,1,0:T(8,128)(2,1)} %copy.39), calls=%async_computation | async-start | bytes 1966080 | tf_op jit(solution)/shard_map/all_to_all | solution.py:19
  (10 other events, 11.3 us)
Sparse Core Ops, SparseCore 0:
  166.6 104.4 all-reduce.5
  296.2 103.1 all-reduce.7
  423.3 103.1 all-reduce.9
  670.4 104.0 all-reduce.11
where the time goes:
time: 795 us; the launch traced here: 784 us
  waiting for transfers between devices  284 us (36%)
  matrix products  188 us (24%)
  other arithmetic  107 us (13%)
  blocking collectives  89.2 us (11%)
  local copies, waits for them, and re-layouts  77.6 us (10%)
  starting transfers between devices  17.1 us (2%)
  between operations  14.7 us (2%)
    psum x1, waiting for transfers between devices, body(): lax.psum(jnp.dot(act_low, down_full, preferred_element_type=jnp.float32)....  103 us
    psum x1, waiting for transfers between devices, body(): lax.psum(hidden_part.astype(jnp.bfloat16), 'mp').astype(jnp.float32)  90.5 us
    psum x1, waiting for transfers between devices, body(): lax.psum(jnp.dot(mixed_low, out_full, preferred_element_type=jnp.float32)...  81.7 us
    dot_general x8, matrix products, scores_at(): jnp.einsum('qhd,khd->hqk', query_block, keys_all, preferred_element_type=...  54.9 us
    psum x1, blocking collectives, body(): lax.psum((padded_qkv, padded_up, out_bias_term, gain_one_term, shift_one_...  44.5 us
    dynamic_update_slice x12, local copies, waits for them, and re-layouts, body(): attended, all_maxima, all_totals = lax.map(attend, jnp.arange(block_count))  38.5 us
    reduce_sum x4, other arithmetic, attend(): totals = jnp.sum(raised, -1, keepdims=True)  27 us
    dot_general x4, matrix products, attend(): jnp.einsum('hqk,khd->qhd', prob_low, values, preferred_element_type=jnp.f...  26.6 us
  transfers between devices with their start and end apart: 8, of which 5 were waited for; matrix products, arithmetic and copies ran while one was open for 23% of the time, Pallas kernels for 0%

commit v1 on v0

--- a/solution.py
+++ b/solution.py
@@ -7,6 +7,11 @@
 HD = 64
 EPS = 1e-05
 SCALE = 0.125
+
+
+def axis_by_axis(array_2, one, other):
+    partial = lax.psum(array_2, one)
+    return lax.psum(partial, other)
 
 
 def cut_along(array, dim, length):
@@ -219,7 +224,7 @@
     padded_up = lax.dynamic_update_slice(
         jnp.zeros((mp_size * hidden_cols,), jnp.float32), bias_up, (mp_index * hidden_cols,)
     )
-    summed = lax.psum(
+    summed = axis_by_axis(
         (
             padded_qkv,
             padded_up,
@@ -230,7 +235,8 @@
             gain_two_term,
             shift_two_term,
         ),
-        ("dp", "mp"),
+        "mp",
+        "dp",
     )
     qkv_bias_grad = lax.dynamic_slice_in_dim(summed[0], mp_index * slot_width, slot_width, 1)
     up_bias_grad = lax.dynamic_slice_in_dim(summed[1], mp_index * hidden_cols, hidden_cols, 0)

time: 795 us -> 796 us (level)
    psum x1 -> x2, blocking collectives: 44.5 us -> 42.9 us  [the longest x1 25 us: axis_by_axis(): return lax.psum(partial, other)]
where the time goes in v1:
time: 796 us; the launch traced here: 786 us
  waiting for transfers between devices  290 us (36%)
  matrix products  192 us (24%)
  other arithmetic  106 us (13%)
  blocking collectives  87.4 us (11%)
  local copies, waits for them, and re-layouts  74.2 us (9%)
  starting transfers between devices  16.3 us (2%)
  between operations  14.6 us (2%)
    psum x1, waiting for transfers between devices, body(): lax.psum(jnp.dot(act_low, down_full, preferred_element_type=jnp.float32)....  103 us
    psum x1, waiting for transfers between devices, body(): lax.psum(hidden_part.astype(jnp.bfloat16), 'mp').astype(jnp.float32)  90.5 us
    psum x1, waiting for transfers between devices, body(): lax.psum(jnp.dot(mixed_low, out_full, preferred_element_type=jnp.float32)...  81.9 us
    dot_general x8, matrix products, scores_at(): jnp.einsum('qhd,khd->hqk', query_block, keys_all, preferred_element_type=...  58.2 us
    dynamic_update_slice x12, local copies, waits for them, and re-layouts, body(): attended, all_maxima, all_totals = lax.map(attend, jnp.arange(block_count))  38.5 us
    reduce_sum x4, other arithmetic, attend(): totals = jnp.sum(raised, -1, keepdims=True)  26.9 us
    dot_general x4, matrix products, attend(): jnp.einsum('hqk,khd->qhd', prob_low, values, preferred_element_type=jnp.f...  26.5 us
    psum x1, blocking collectives, axis_by_axis(): return lax.psum(partial, other)  25 us
  transfers between devices with their start and end apart: 8, of which 5 were waited for; matrix products, arithmetic and copies ran while one was open for 23% of the time, Pallas kernels for 0%

profile of v1, /device:TPU:0, one launch (start us, length us, event | category | flops | bytes accessed | tf_op | source)
XLA Modules:
  0.0 785.6 jit_solution(12784784941886100501)
XLA Ops:
  8.2 11.1 %all_gather.13 = bf16[192,640]{0,1:T(8,128)(2,1)S(1)} all-gather(bf16[192,80]{0,1:T(8,128)(2,1)} %param.23), channel_id=1, replica_groups=mesh['dp'=8,'mp'=4] {'dp'}, dimensions={1}, use_global_device_ids=true | all-gather | bytes 276480 | tf_op jit(solution)/shard_map/all_gather | solution.py:67
  19.3 10.8 %all_gather.12 = bf16[3,640,192]{2,1,0:T(8,128)(2,1)S(1)} all-gather(bf16[3,80,192]{2,1,0:T(8,128)(2,1)} %param.21), channel_id=1, replica_groups=mesh['dp'=8,'mp'=4] {'dp'}, dimensions={1}, use_global_device_ids=true | all-gather | bytes 829440 | tf_op jit(solution)/shard_map/all_gather | solution.py:66
  30.2 4.4 fusion.38
  35.8 127.1 %while.29 = (s32[]{:T(128)}, f32[4,512,3,64]{1,0,3,2:T(4,128)}, f32[4,3,512,1]{2,1,3,0:T(4,128)}, f32[4,3,512,1]{2,1,3,0:T(4,128)S(1)}, s32[4]{0:T(128)S(1)}, /*...) while((s32[]{:T(128)}, f32[4,512,3,64]{1,0,3,2:T(4,128)}, ...), condition=%wide.region_3.4_spmd, body=%wide.region_0.3_spmd.sunk | while | flops 844100608 | bytes 45756624 | solution.py:113
  37.8 6.8 fusion.104
  44.6 6.7 fusion.105
  51.3 6.6 fusion.106
  59.0 8.6 %dynamic_update_slice.30 = f32[4,512,3,64]{1,0,3,2:T(4,128)} dynamic-update-slice(f32[4,512,3,64]{1,0,3,2:T(4,128)} %get-tuple-element.421, f32[1,512,3,64]{1,0,3,2:T(1,128)S(1)} %copy.68, s32[]{:T(128)S(6)} %copy.77, s32[]{:T(128)} %constant.76.clone.1..sunk, s32[]{:T(128)} %constant.76.clone.1..sunk, s32[]{:T(128)} %constant.76.clone.1..sunk) | dynamic-update-slice | bytes 786436 | tf_op jit(solution)/shard_map/while/body/jit(dynamic_update_index_in_dim)/dynamic_update_slice | solution.py:113
  69.6 6.8 fusion.104
  76.4 6.7 fusion.105
  83.1 6.6 fusion.106
  90.7 8.6 %dynamic_update_slice.30 = f32[4,512,3,64]{1,0,3,2:T(4,128)} dynamic-update-slice(f32[4,512,3,64]{1,0,3,2:T(4,128)} %get-tuple-element.421, f32[1,512,3,64]{1,0,3,2:T(1,128)S(1)} %copy.68, s32[]{:T(128)S(6)} %copy.77, s32[]{:T(128)} %constant.76.clone.1..sunk, s32[]{:T(128)} %constant.76.clone.1..sunk, s32[]{:T(128)} %constant.76.clone.1..sunk) | dynamic-update-slice | bytes 786436 | tf_op jit(solution)/shard_map/while/body/jit(dynamic_update_index_in_dim)/dynamic_update_slice | solution.py:113
  101.3 6.8 fusion.104
  108.1 6.7 fusion.105
  114.9 6.6 fusion.106
  122.5 8.6 %dynamic_update_slice.30 = f32[4,512,3,64]{1,0,3,2:T(4,128)} dynamic-update-slice(f32[4,512,3,64]{1,0,3,2:T(4,128)} %get-tuple-element.421, f32[1,512,3,64]{1,0,3,2:T(1,128)S(1)} %copy.68, s32[]{:T(128)S(6)} %copy.77, s32[]{:T(128)} %constant.76.clone.1..sunk, s32[]{:T(128)} %constant.76.clone.1..sunk, s32[]{:T(128)} %constant.76.clone.1..sunk) | dynamic-update-slice | bytes 786436 | tf_op jit(solution)/shard_map/while/body/jit(dynamic_update_index_in_dim)/dynamic_update_slice | solution.py:113
  133.1 6.8 fusion.104
  139.9 6.7 fusion.105
  146.7 6.6 fusion.106
  154.3 8.6 %dynamic_update_slice.30 = f32[4,512,3,64]{1,0,3,2:T(4,128)} dynamic-update-slice(f32[4,512,3,64]{1,0,3,2:T(4,128)} %get-tuple-element.421, f32[1,512,3,64]{1,0,3,2:T(1,128)S(1)} %copy.68, s32[]{:T(128)S(6)} %copy.77, s32[]{:T(128)} %constant.76.clone.1..sunk, s32[]{:T(128)} %constant.76.clone.1..sunk, s32[]{:T(128)} %constant.76.clone.1..sunk) | dynamic-update-slice | bytes 786436 | tf_op jit(solution)/shard_map/while/body/jit(dynamic_update_index_in_dim)/dynamic_update_slice | solution.py:113
  168.3 10.6 %all_gather.14 = bf16[640,560]{1,0:T(8,128)(2,1)S(1)} all-gather(bf16[80,560]{1,0:T(8,128)(2,1)} %param.27), channel_id=1, replica_groups=mesh['dp'=8,'mp'=4] {'dp'}, dimensions={0}, use_global_device_ids=true | all-gather | bytes 806400 | tf_op jit(solution)/shard_map/all_gather | solution.py:68
  178.9 12.0 %all_gather.15 = bf16[560,640]{0,1:T(8,128)(2,1)} all-gather(bf16[560,80]{0,1:T(8,128)(2,1)} %param.29), channel_id=1, replica_groups=mesh['dp'=8,'mp'=4] {'dp'}, dimensions={1}, use_global_device_ids=true | all-gather | bytes 806400 | tf_op jit(solution)/shard_map/all_gather | solution.py:69
  190.9 81.9 %all-reduce.7.cloned.1.call-done = bf16[2048,640]{1,0:T(8,128)(2,1)} async-done(((bf16[2048,640]{1,0:T(8,128)(2,1)}), bf16[2048,640]{1,0:T(8,128)(2,1)}) %all-reduce.7.cloned.1.call-update) | async-done | bytes 2621456 | tf_op jit(solution)/shard_map/psum | solution.py:121
  272.8 3.6 fusion.37
  279.6 13.4 %multiply_convert_fusion.1 = (bf16[2048,560]{0,1:T(8,128)(2,1)S(1)}, f32[2048,560]{0,1:T(8,128)}, f32[2048,560]{0,1:T(8,128)}) fusion(f32[560]{0:T(1024)S(1)} %copy-done.39, bf16[640,560]{1,0:T(8,128)(2,1)S(1)} %all_gather.14, f32[2048,640]{1,0:T(8,128)S(1)} %subtract_multiply_fusion.3, f32[640]{0:T(1024)S(1)} %copy-done.31, f32[640]{0:T(1024)S(1)} %copy-done.26), kind=kOutput, calls=%fused_computation.61 | convolution fusion | flops 1547632640 | bytes 17435840 | tf_op jit(solution)/shard_map/dot_general | solution.py:128
  294.4 4.0 convolution_convert_fusion.1
  298.7 103.0 %all-reduce.9.cloned.1.call-done = bf16[2048,640]{1,0:T(8,128)(2,1)} async-done(((bf16[2048,640]{1,0:T(8,128)(2,1)}), bf16[2048,640]{1,0:T(8,128)(2,1)}) %all-reduce.9.cloned.1.call-update) | async-done | bytes 2621456 | tf_op jit(solution)/shard_map/psum | solution.py:130
  401.7 4.5 fusion.52
  406.3 3.5 multiply_reduce_fusion.3
  415.8 4.5 convert_reduce_fusion
  421.7 4.0 convolution_convert_fusion
  426.2 5.3 convolution_convert_fusion.5
  433.7 4.2 all-to-all-start.3
  438.4 90.5 %all-reduce.11.cloned.1.call-done = bf16[2048,640]{1,0:T(8,128)(2,1)} async-done(((bf16[2048,640]{1,0:T(8,128)(2,1)}), bf16[2048,640]{1,0:T(8,128)(2,1)}) %all-reduce.11.cloned.1.call-update) | async-done | bytes 2621456 | tf_op jit(solution)/shard_map/psum | solution.py:149
  528.9 6.9 multiply_reduce_fusion.5
  535.9 6.6 fusion.57
  546.1 115.1 %while.30 = (s32[]{:T(128)}, f32[2048,3,64]{0,2,1:T(8,128)S(1)}, f32[2048,3,64]{0,2,1:T(8,128)S(1)}, bf16[4,512,3,64]{1,3,2,0:T(8,128)(2,1)}, s32[4]{0:T(128)S(1...) while((s32[]{:T(128)}, f32[2048,3,64]{0,2,1:T(8,128)S(1)}, ...), condition=%wide.region_17.18_spmd.clone, body=%wide.region_15.17_spmd.clone.sunk | while | flops 2047834624 | bytes 118950256 | solution.py:189
  548.8 3.2 fusion.116
  552.0 7.8 multiply_reduce_fusion.10
  559.8 5.5 multiply_convert_fusion.6
  565.3 6.2 fusion.118
  577.6 3.2 fusion.116
  580.8 7.8 multiply_reduce_fusion.10
  588.6 5.5 multiply_convert_fusion.6
  594.1 6.2 fusion.118
  606.4 3.2 fusion.116
  609.6 7.8 multiply_reduce_fusion.10
  617.4 5.5 multiply_convert_fusion.6
  622.9 6.2 fusion.118
  635.2 3.2 fusion.116
  638.4 7.8 multiply_reduce_fusion.10
  646.2 5.5 multiply_convert_fusion.6
  651.6 6.2 fusion.118
  668.9 4.0 bitcast_convert_fusion
  672.9 5.1 convolution_convert_fusion.4
  679.3 3.8 all-to-all-start.2
  683.1 4.4 convert_element_type.151
  692.8 3.2 all-to-all-done.2
  700.4 3.4 all-to-all-start.1
  703.9 4.8 fusion.46
  711.4 4.1 all-to-all-start
  719.5 18.0 %all-reduce.1 = (f32[2,768]{1,0:T(2,128)S(1)}, f32[640]{0:T(1024)S(1)}, f32[640]{0:T(1024)S(1)}, f32[640]{0:T(1024)S(1)}, f32[2240]{0:T(1024)S(1)}, /*index=5*/f...) all-reduce(f32[2,768]{1,0:T(2,128)S(1)} %dynamic_update_slice.20, ...), channel_id=1, replica_groups=mesh['dp'=8,'mp'=4] {'mp'}, use_global_device_ids=true, to_apply=%region_22.23 | all-reduce | flops 7616 | bytes 60928 | tf_op jit(solution)/shard_map/psum | solution.py:13
  737.5 25.0 %all-reduce = (f32[2,768]{1,0:T(2,128)S(1)}, f32[640]{0:T(1024)}, f32[640]{0:T(1024)}, f32[640]{0:T(1024)}, f32[2240]{0:T(1024)S(1)}, /*index=5*/f32[640]{0:T(1024)}, f32[640]{0:T(1024)}, f32[640]{0:T(1024)}) all-reduce(f32[2,768]{1,0:T(2,128)S(1)} %get-tuple-element.230, ...), channel_id=1, replica_groups=mesh['dp'=8,'mp'=4] {'dp'}, use_global_device_ids=true, to_apply=%region_23.24 | all-reduce | flops 7616 | bytes 60928 | tf_op jit(solution)/shard_map/psum | solution.py:14
  765.3 11.1 %all-reduce.13.cloned.1.call-done = bf16[2048,640]{1,0:T(8,128)(2,1)} async-done(((bf16[2048,640]{1,0:T(8,128)(2,1)}), bf16[2048,640]{1,0:T(8,128)(2,1)}) %all-reduce.13.cloned.1.call-update) | async-done | bytes 2621456 | tf_op jit(solution)/shard_map/psum | solution.py:204
  (237 shorter events, 88.0 us)
Async XLA Ops:
  7.2 265.6 %all-reduce.7.cloned.1.call-start = ((), (), s32[]{:S(2)}) async-start(), calls=%async_computation.4 | async-start | bytes 5242880 | tf_op jit(solution)/shard_map/psum | solution.py:121
  7.4 158.1 %copy-start.34 = (f32[192]{0:T(256)}, f32[192]{0:T(256)S(1)}, u32[]{:S(2)}) copy-start(f32[192]{0:T(256)S(1)} %mul.192) | copy-start | bytes 2308
  30.1 4.6 copy-start.20
  162.9 5.3 copy-start.2
  162.9 5.3 copy-start.4
  165.5 110.9 %copy-start.11 = (f32[24,8,4,512]{3,1,2,0:T(8,128)}, f32[24,8,4,512]{3,1,2,0:T(8,128)S(1)}, u32[]{:S(2)}) copy-start(f32[24,8,4,512]{3,1,2,0:T(8,128)S(1)} %copy.66) | copy-start | bytes 4718596
  165.5 107.3 %copy-start.33 = (f32[640]{0:T(1024)S(1)}, f32[640]{0:T(1024)}, u32[]{:S(2)}) copy-start(f32[640]{0:T(1024)} %param.24) | copy-start | bytes 7684
  168.3 233.5 %all-reduce.9.cloned.1.call-start = ((), (), s32[]{:S(2)}) async-start(), calls=%async_computation.5 | async-start | bytes 5242880 | tf_op jit(solution)/shard_map/psum | solution.py:130
  272.8 3.6 copy-start.9
  272.8 4.1 copy-start.10
  278.4 1.2 copy-start.26
  278.4 1.2 copy-start.31
  279.6 13.4 %copy-start = (f32[2048,640]{1,0:T(8,128)}, f32[2048,640]{1,0:T(8,128)S(1)}, u32[]{:S(2)}) copy-start(f32[2048,640]{1,0:T(8,128)S(1)} %subtract_multiply_fusion.3) | copy-start | bytes 15728644
  279.6 14.8 %copy-start.22 = (bf16[560,640]{0,1:T(8,128)(2,1)S(1)}, bf16[560,640]{0,1:T(8,128)(2,1)}, u32[]{:S(2)}) copy-start(bf16[560,640]{0,1:T(8,128)(2,1)} %all_gather.15) | copy-start | bytes 2150404
  293.0 1.4 copy-start.40
  294.4 107.3 %copy-start.30 = (f32[640]{0:T(1024)S(1)}, f32[640]{0:T(1024)}, u32[]{:S(2)}) copy-start(f32[640]{0:T(1024)} %param.30) | copy-start | bytes 7684
  298.5 230.4 %all-reduce.11.cloned.1.call-start = ((), (), s32[]{:S(2)}) async-start(), calls=%async_computation.6 | async-start | bytes 5242880 | tf_op jit(solution)/shard_map/psum | solution.py:149
  401.7 4.6 copy-start.8
  401.7 8.1 %slice-start = ((s8[5242880]{0:T(1024)(128)(4,1)}), s8[1048576]{0:T(1024)(128)(4,1)S(1)}, s32[]{:S(2)}) async-start(s8[5242880]{0:T(1024)(128)(4,1)} %bitcast.122), calls=%async_computation.8 | async-start | bytes 2097152
  406.3 3.6 copy-start.3
  406.3 3.6 copy-start.28
  406.3 4.5 slice-start.1
  406.3 9.4 %slice-start.2 = ((s8[4587520]{0:T(1024)(128)(4,1)}), s8[4194304]{0:T(1024)(128)(4,1)S(1)}, s32[]{:S(2)}) async-start(s8[4587520]{0:T(1024)(128)(4,1)} %bitcast.140), calls=%async_computation.10 | async-start | bytes 8388608
  406.3 9.4 %slice-start.4 = ((s8[4587520]{0:T(1024)(128)(4,1)}), s8[4194304]{0:T(1024)(128)(4,1)S(1)}, s32[]{:S(2)}) async-start(s8[4587520]{0:T(1024)(128)(4,1)} %bitcast.142), calls=%async_computation.12 | async-start | bytes 8388608
  410.9 4.9 slice-start.3
  410.9 4.9 slice-start.5
  413.3 2.4 copy-start.1
  415.7 4.6 copy-start.13
  420.3 1.4 copy-start.41
  433.7 245.6 %all-to-all-start.3 = ((bf16[8,560,80]{1,2,0:T(8,128)(2,1)}), bf16[8,560,80]{1,2,0:T(8,128)(2,1)}, u32[]{:S(2)}, u32[]{:S(2)}) async-start(bf16[8,560,80]{1,2,0:T(8,128)(2,1)} %bitcast.130), calls=%async_computation.3 | async-start | bytes 1638400 | tf_op jit(solution)/shard_map/all_to_all | solution.py:24
  438.0 338.4 %all-reduce.13.cloned.1.call-start = ((), (), s32[]{:S(2)}) async-start(), calls=%async_computation.7 | async-start | bytes 5242880 | tf_op jit(solution)/shard_map/psum | solution.py:204
  535.9 6.6 copy-start.7
  535.9 9.2 %copy-start.38 = (bf16[3]{0:T(256)(128)(2,1)S(1)}, bf16[3]{0:T(256)(128)(2,1)}, u32[]{:S(2)}) copy-start(bf16[3]{0:T(256)(128)(2,1)} %fusion.55) | copy-start | bytes 22
  542.5 1.5 copy-start.6
  548.8 3.2 copy-start.5
  548.8 3.2 copy-start.14
  565.3 6.2 copy-start.23
  573.5 1.4 copy-start.24
  577.6 3.2 copy-start.5
  577.6 3.2 copy-start.14
  594.0 6.2 copy-start.23
  602.3 1.4 copy-start.24
  606.4 3.2 copy-start.5
  606.4 3.2 copy-start.14
  622.8 6.2 copy-start.23
  631.1 1.4 copy-start.24
  635.2 3.2 copy-start.5
  635.2 3.2 copy-start.14
  651.6 6.2 copy-start.23
  659.9 1.4 copy-start.24
  666.9 1.4 copy-start.15
  666.9 2.0 copy-start.21
  668.9 4.0 copy-start.27
  668.9 4.0 copy-start.32
  679.3 8.2 %copy-start.37 = (f32[560]{0:T(1024)S(1)}, f32[560]{0:T(1024)}, u32[]{:S(2)}) copy-start(f32[560]{0:T(1024)} %get-tuple-element.238) | copy-start | bytes 6724
  679.3 8.5 %copy-start.29 = (f32[640]{0:T(1024)S(1)}, f32[640]{0:T(1024)}, u32[]{:S(2)}) copy-start(f32[640]{0:T(1024)} %param.31) | copy-start | bytes 7684
  679.3 8.5 %copy-start.36 = (f32[640]{0:T(1024)S(1)}, f32[640]{0:T(1024)}, u32[]{:S(2)}) copy-start(f32[640]{0:T(1024)} %param.32) | copy-start | bytes 7684
  679.3 16.7 %all-to-all-start.2 = ((bf16[8,80,560]{2,1,0:T(8,128)(2,1)}), bf16[8,80,560]{2,1,0:T(8,128)(2,1)S(1)}, u32[]{:S(2)}, u32[]{:S(2)}) async-start(bf16[8,80,560]{2,1,0:T(8,128)(2,1)} %bitcast.21), calls=%async_computation.2 | async-start | bytes 1638400 | tf_op jit(solution)/shard_map/all_to_all | solution.py:24
  687.5 9.4 %copy-start.12 = (f32[24,8,4,512]{3,1,2,0:T(8,128)S(1)}, f32[24,8,4,512]{3,1,2,0:T(8,128)}, u32[]{:S(2)}) copy-start(f32[24,8,4,512]{3,1,2,0:T(8,128)} %copy-done.11) | copy-start | bytes 4718596
  687.5 9.4 %copy-start.35 = (f32[192]{0:T(256)S(1)}, f32[192]{0:T(256)}, u32[]{:S(2)}) copy-start(f32[192]{0:T(256)} %copy-done.34) | copy-start | bytes 2308
  690.8 13.1 %copy-start.16 = (bf16[1,2048,192]{1,2,0:T(8,128)(2,1)S(1)}, bf16[1,2048,192]{1,2,0:T(8,128)(2,1)}, u32[]{:S(2)}) copy-start(bf16[1,2048,192]{1,2,0:T(8,128)(2,1)} %stack.24) | copy-start | bytes 2359300
  696.9 7.0 copy-start.18
  700.4 11.0 %all-to-all-start.1 = ((bf16[8,192,80]{1,2,0:T(8,128)(2,1)}), bf16[8,192,80]{1,2,0:T(8,128)(2,1)S(1)}, u32[]{:S(2)}, u32[]{:S(2)}) async-start(bf16[8,192,80]{1,2,0:T(8,128)(2,1)} %bitcast.20), calls=%async_computation.1 | async-start | bytes 655360 | tf_op jit(solution)/shard_map/all_to_all | solution.py:24
  711.4 53.0 %all-to-all-start = ((bf16[8,3,80,192]{3,2,1,0:T(8,128)(2,1)}), bf16[8,3,80,192]{3,2,1,0:T(8,128)(2,1)S(1)}, u32[]{:S(2)}, u32[]{:S(2)}) async-start(bf16[8,3,80,192]{3,2,1,0:T(8,128)(2,1)} %copy.39), calls=%async_computation | async-start | bytes 1966080 | tf_op jit(solution)/shard_map/all_to_all | solution.py:24
  (4 other events, 4.2 us)
Sparse Core Ops, SparseCore 0:
  168.4 104.4 all-reduce.6
  298.6 103.1 all-reduce.8
  425.8 103.1 all-reduce.10
  673.0 103.3 all-reduce.12
